TPU v7x, 128 devices: a whole 4x4x4 slice. The times are simulated.
128 devices in a mesh: fsdp: 16 (over z, x_lo, core), rows: 8 (over y, x_hi).
Axes of the slice: x: 4 (x_hi: 2, x_lo: 2; x = x_hi * 2 + x_lo), y: 4, z: 4, core: 2. Of those that a mesh axis runs over, the one named last changes fastest.
Arguments:
- query_rows: bfloat16 [16, 2048, 1536], P('fsdp', 'rows'), may hold values from -6 to 6
- key_rows: bfloat16 [16, 2048, 1536], P('fsdp', 'rows'), may hold values from -6 to 6
- value_rows: bfloat16 [16, 2048, 1536], P('fsdp', 'rows'), may hold values from -6 to 6
- grad_out: bfloat16 [16, 2048, 3072], P('fsdp', 'rows'), may hold values from -6 to 6
- w_out: bfloat16 [1536, 3072], P('fsdp'), may hold values from -0.15625 to 0.15625
Outputs:
- grad_query: bfloat16 [16, 2048, 1536], P('fsdp', 'rows')
- grad_key: bfloat16 [16, 2048, 1536], P('fsdp', 'rows')
- grad_value: bfloat16 [16, 2048, 1536], P('fsdp', 'rows')
- grad_w_out: float32 [1536, 3072], P('fsdp')
All inputs are finite; a program needn't handle non-finite values.
Results may differ from a plain program's by a relative error of at most 0.02.
Values may be sent and summed in bfloat16 or wider, within the bound.
A program may use at most 192 MiB of HBM per device.

v0:
```python
import math
import jax
import jax.numpy as jnp
from jax import lax
from jax.sharding import PartitionSpec as P

HDIM = 128
HEADS = 12
HW = 1536


def in_one_piece(arrays, axis, dim, along):
    both = jnp.concatenate(arrays, axis=along)
    result, at, outs = (lax.all_gather(both, axis, axis=dim, tiled=True), 0, [])
    for a in arrays:
        outs.append(lax.slice_in_dim(result, at, at + a.shape[along], axis=along))
        at += a.shape[along]
    return tuple(outs)


def cut_along(array, dim, devices):
    shape = array.shape
    tiles = array.reshape(*shape[:dim], devices, shape[dim] // devices, *shape[dim + 1 :])
    return jnp.moveaxis(tiles, dim, 0)


def sent_and_summed(array, axis, dim):
    devices = lax.axis_size(axis)
    tiles = lax.all_to_all(cut_along(array, dim, devices), axis, 0, 0, tiled=True)
    return jnp.sum(tiles.astype(jnp.float32), axis=0)


def in_one_piece_2(arrays, axis, dim, along):
    ends, at = ([], 0)
    for a in arrays[:-1]:
        at += a.shape[along]
        ends.append(at)
    both = jnp.concatenate(arrays, axis=along)
    return tuple(jnp.split(sent_and_summed(both, axis, dim), ends, axis=along))


def split_heads(array, count, groups):
    per_group = HEADS // groups
    return jnp.moveaxis(array.reshape(count, groups, per_group, HDIM), 1, 0)


def join_heads(array, count):
    return jnp.moveaxis(array, 0, 1).reshape(count, HW)


def local(query_rows, key_rows, value_rows, grad_out, w_out):
    tokens = query_rows.shape[1]
    factor = 1.0 / math.sqrt(HDIM)
    grad_flat = grad_out[0]
    groups = HEADS // 4
    grad_attn = lax.dot_general(
        grad_flat,
        lax.all_gather(w_out, "fsdp", axis=0, tiled=True),
        (((1,), (1,)), ((), ())),
        preferred_element_type=jnp.float32,
    ).astype(jnp.bfloat16)
    all_keys, all_values = in_one_piece((key_rows, value_rows), "rows", 1, 0)
    length = all_keys.shape[1]

    def attend(inputs):
        query_heads, key_heads, value_heads, grad_heads = inputs
        scores = (
            jnp.einsum("qhd,khd->hqk", query_heads, key_heads, preferred_element_type=jnp.float32)
            * factor
        )
        probs = jax.nn.softmax(scores, axis=-1)
        probs_low = probs.astype(jnp.bfloat16)
        attended = jnp.einsum(
            "hqk,khd->qhd", probs_low, value_heads, preferred_element_type=jnp.float32
        )
        value_part = jnp.einsum(
            "hqk,qhd->khd", probs_low, grad_heads, preferred_element_type=jnp.float32
        )
        grad_probs = jnp.einsum(
            "qhd,khd->hqk", grad_heads, value_heads, preferred_element_type=jnp.float32
        )
        centre = jnp.sum(probs * grad_probs, axis=-1, keepdims=True)
        grad_scores = (probs * (grad_probs - centre)).astype(jnp.bfloat16)
        grad_query = (
            jnp.einsum("hqk,khd->qhd", grad_scores, key_heads, preferred_element_type=jnp.float32)
            * factor
        )
        key_part = (
            jnp.einsum("hqk,qhd->khd", grad_scores, query_heads, preferred_element_type=jnp.float32)
            * factor
        )
        return (
            attended.astype(jnp.bfloat16),
            grad_query.astype(jnp.bfloat16),
            key_part,
            value_part,
        )

    attended, grad_query, key_part, value_part = lax.map(
        attend,
        (
            split_heads(query_rows[0], tokens, groups),
            split_heads(all_keys[0], length, groups),
            split_heads(all_values[0], length, groups),
            split_heads(grad_attn, tokens, groups),
        ),
    )
    attended = join_heads(attended, tokens)
    grad_query = join_heads(grad_query, tokens).reshape(1, tokens, HW)
    key_part = join_heads(key_part, length)
    value_part = join_heads(value_part, length)
    grad_key, grad_value = in_one_piece_2(
        (
            key_part.reshape(1, length, HW).astype(jnp.bfloat16),
            value_part.reshape(1, length, HW).astype(jnp.bfloat16),
        ),
        "rows",
        1,
        0,
    )
    term = lax.dot_general(
        attended, grad_flat, (((0,), (0,)), ((), ())), preferred_element_type=jnp.float32
    )
    partial_grad = sent_and_summed(
        lax.optimization_barrier(term.astype(jnp.bfloat16))
        .astype(jnp.float32)
        .astype(jnp.bfloat16),
        "fsdp",
        0,
    )
    grad_w_out = lax.psum(partial_grad.astype(jnp.bfloat16), "rows").astype(jnp.float32)
    return (grad_query, grad_key.astype(jnp.bfloat16), grad_value.astype(jnp.bfloat16), grad_w_out)


def solution(mesh):
    in_specs = (
        P("fsdp", "rows", None),
        P("fsdp", "rows", None),
        P("fsdp", "rows", None),
        P("fsdp", "rows", None),
        P("fsdp", None),
    )
    out_specs = (
        P("fsdp", "rows", None),
        P("fsdp", "rows", None),
        P("fsdp", "rows", None),
        P("fsdp", None),
    )
    return jax.shard_map(local, mesh=mesh, in_specs=in_specs, out_specs=out_specs, check_vma=False)
```

profile of v0, /device:TPU:0, one launch (start us, length us, event | category | flops | bytes accessed | tf_op | source)
XLA Modules:
  0.0 665.3 jit_solution(4083551851996054782)
XLA Ops:
  8.0 1.4 copy.45
  9.4 1.4 copy.46
  10.8 1.3 pad_maximum_fusion
  12.2 1.4 copy.47
  13.6 55.7 %all-gather.5.cloned.1.call-done = bf16[1536,3072]{1,0:T(8,128)(2,1)} async-done(((bf16[96,3072]{1,0:T(8,128)(2,1)}), bf16[1536,3072]{1,0:T(8,128)(2,1)}) %all-gather.5.cloned.1.call-update) | async-done | bytes 9437200 | tf_op jit(solution)/shard_map/all_gather | solution.py:58
  69.3 7.2 %convolution_convert_fusion.1 = bf16[256,1536]{1,0:T(8,128)(2,1)} fusion(bf16[1536,3072]{1,0:T(8,128)(2,1)} %all-gather.5.cloned.1.call-done, bf16[1,256,3072]{2,1,0:T(8,128)(2,1)S(1)} %copy-done), kind=kOutput, calls=%fused_computation.48 | convolution fusion | flops 2416312320 | bytes 11796480 | tf_op jit(solution)/shard_map/dot_general | solution.py:56
  76.5 1.7 reshape.51
  79.3 146.3 %all-gather.3.cloned.1.call-done = bf16[2,2048,1536]{1,2,0:T(8,128)(2,1)} async-done(((bf16[2,256,1536]{1,2,0:T(8,128)(2,1)}), bf16[2,2048,1536]{1,2,0:T(8,128)(2,1)}) %all-gather.3.cloned.1.call-update) | async-done | bytes 12582928 | tf_op jit(solution)/shard_map/all_gather | solution.py:14
  225.6 10.6 %fusion.72 = (bf16[1,2048,1536]{1,2,0:T(8,128)(2,1)}, bf16[1,2048,1536]{1,2,0:T(8,128)(2,1)}) fusion(bf16[2,2048,1536]{1,2,0:T(8,128)(2,1)} %all-gather.3.cloned.1.call-done), kind=kLoop, calls=%fused_computation.54 | loop fusion | bytes 25165824 | tf_op jit(solution)/shard_map/slice | solution.py:16
  236.3 125.0 %while.16 = (s32[]{:T(128)}, bf16[3,256,4,128]{1,3,2,0:T(8,128)(2,1)S(1)}, bf16[3,256,4,128]{1,3,2,0:T(8,128)(2,1)}, bf16[3,2048,4,128]{1,3,2,0:T(8,128)(2,1)}, ...) while((s32[]{:T(128)}, ...), condition=%wide.region_4.5_spmd, body=%wide.region_0.4_spmd.sunk | while | flops 3266714624 | bytes 190351520 | solution.py:99
  236.3 2.9 fusion.106
  239.2 4.6 fusion.107
  244.9 9.1 %fusion.108 = bf16[3,256,4,128]{1,3,2,0:T(8,128)(2,1)S(1)} fusion(bf16[3,256,4,128]{1,3,2,0:T(8,128)(2,1)S(1)} %get-tuple-element.193, s32[]{:T(128)S(6)} %copy.79, bf16[3,2048,4,128]{1,3,2,0:T(8,128)(2,1)} %get-tuple-element.207, f32[4,256]{1,0:T(4,128)S(1)} %get-tuple-element.178, f32[4,256,2048]{2,1,0:T(8,128)} %copy-done.1), kind=kOutput, calls=%fused_computation.30.clone.1 | convolution fusion | flops 547490816 | bytes 19141632 | tf_op jit(solution)/shard_map/while/body/eval_jaxpr/hqk,khd->qhd/dot_general | solution.py:73
  254.0 10.0 %bitcast_dynamic-update-slice_fusion.5 = bf16[3,2048,4,128]{1,3,2,0:T(8,128)(2,1)} fusion(bf16[3,2048,4,128]{1,3,2,0:T(8,128)(2,1)} %get-tuple-element.196, s32[]{:T(128)S(6)} %copy.79, bf16[3,256,4,128]{3,1,2,0:T(8,128)(2,1)} %get-tuple-element.210, f32[4,256]{1,0:T(4,128)S(1)} %get-tuple-element.178, f32[4,256,2048]{2,1,0:T(8,128)} %copy-done.1), kind=kOutput, calls=%fused_computation.6.clone.1 | convolution fusion | flops 547359744 | bytes 21238784 | tf_op jit(solution)/shard_map/while/body/eval_jaxpr/hqk,qhd->khd/dot_general | solution.py:76
  264.1 5.6 multiply_reduce_fusion.3
  270.5 1.4 multiply_convert_fusion.2
  271.9 3.8 fusion.109
  275.8 2.2 bitcast_dynamic-update-slice_fusion.4
  277.9 2.9 fusion.106
  280.8 4.6 fusion.107
  286.6 9.1 %fusion.108 = bf16[3,256,4,128]{1,3,2,0:T(8,128)(2,1)S(1)} fusion(bf16[3,256,4,128]{1,3,2,0:T(8,128)(2,1)S(1)} %get-tuple-element.193, s32[]{:T(128)S(6)} %copy.79, bf16[3,2048,4,128]{1,3,2,0:T(8,128)(2,1)} %get-tuple-element.207, f32[4,256]{1,0:T(4,128)S(1)} %get-tuple-element.178, f32[4,256,2048]{2,1,0:T(8,128)} %copy-done.1), kind=kOutput, calls=%fused_computation.30.clone.1 | convolution fusion | flops 547490816 | bytes 19141632 | tf_op jit(solution)/shard_map/while/body/eval_jaxpr/hqk,khd->qhd/dot_general | solution.py:73
  295.7 10.1 %bitcast_dynamic-update-slice_fusion.5 = bf16[3,2048,4,128]{1,3,2,0:T(8,128)(2,1)} fusion(bf16[3,2048,4,128]{1,3,2,0:T(8,128)(2,1)} %get-tuple-element.196, s32[]{:T(128)S(6)} %copy.79, bf16[3,256,4,128]{3,1,2,0:T(8,128)(2,1)} %get-tuple-element.210, f32[4,256]{1,0:T(4,128)S(1)} %get-tuple-element.178, f32[4,256,2048]{2,1,0:T(8,128)} %copy-done.1), kind=kOutput, calls=%fused_computation.6.clone.1 | convolution fusion | flops 547359744 | bytes 21238784 | tf_op jit(solution)/shard_map/while/body/eval_jaxpr/hqk,qhd->khd/dot_general | solution.py:76
  305.8 5.6 multiply_reduce_fusion.3
  312.3 1.4 multiply_convert_fusion.2
  313.7 3.8 fusion.109
  317.5 2.1 bitcast_dynamic-update-slice_fusion.4
  319.6 2.9 fusion.106
  322.5 4.6 fusion.107
  328.3 9.1 %fusion.108 = bf16[3,256,4,128]{1,3,2,0:T(8,128)(2,1)S(1)} fusion(bf16[3,256,4,128]{1,3,2,0:T(8,128)(2,1)S(1)} %get-tuple-element.193, s32[]{:T(128)S(6)} %copy.79, bf16[3,2048,4,128]{1,3,2,0:T(8,128)(2,1)} %get-tuple-element.207, f32[4,256]{1,0:T(4,128)S(1)} %get-tuple-element.178, f32[4,256,2048]{2,1,0:T(8,128)} %copy-done.1), kind=kOutput, calls=%fused_computation.30.clone.1 | convolution fusion | flops 547490816 | bytes 19141632 | tf_op jit(solution)/shard_map/while/body/eval_jaxpr/hqk,khd->qhd/dot_general | solution.py:73
  337.4 10.0 %bitcast_dynamic-update-slice_fusion.5 = bf16[3,2048,4,128]{1,3,2,0:T(8,128)(2,1)} fusion(bf16[3,2048,4,128]{1,3,2,0:T(8,128)(2,1)} %get-tuple-element.196, s32[]{:T(128)S(6)} %copy.79, bf16[3,256,4,128]{3,1,2,0:T(8,128)(2,1)} %get-tuple-element.210, f32[4,256]{1,0:T(4,128)S(1)} %get-tuple-element.178, f32[4,256,2048]{2,1,0:T(8,128)} %copy-done.1), kind=kOutput, calls=%fused_computation.6.clone.1 | convolution fusion | flops 547359744 | bytes 21238784 | tf_op jit(solution)/shard_map/while/body/eval_jaxpr/hqk,qhd->khd/dot_general | solution.py:76
  347.4 5.6 multiply_reduce_fusion.3
  353.9 1.4 multiply_convert_fusion.2
  355.2 3.8 fusion.109
  359.1 2.2 bitcast_dynamic-update-slice_fusion.4
  361.2 5.1 convolution_convert_fusion
  366.3 4.8 all-to-all-start.1
  371.1 5.5 copy.67
  376.6 5.5 copy.66
  383.4 7.8 %copy.52 = bf16[8,2,256,1536]{2,3,1,0:T(8,128)(2,1)} copy(bf16[8,2,256,1536]{2,0,3,1:T(8,128)(2,1)S(1)} %maximum_bitcast_fusion) | data formatting | bytes 25165824 | tf_op jit(solution)/shard_map/transpose | solution.py:24
  391.2 86.4 %all-to-all-done.1 = bf16[16,96,3072]{2,1,0:T(8,128)(2,1)} async-done(((bf16[16,96,3072]{2,1,0:T(8,128)(2,1)}), bf16[16,96,3072]{2,1,0:T(8,128)(2,1)}, u32[]{:S(2)}, u32[]{:S(2)}) %all-to-all-start.1) | async-done | bytes 9437216 | tf_op jit(solution)/shard_map/all_to_all | solution.py:29
  477.7 5.4 all-to-all-start
  483.4 6.5 reduce_sum.40
  491.1 93.4 %all-reduce.2.cloned.1.call-done = bf16[96,3072]{1,0:T(8,128)(2,1)} async-done(((bf16[96,3072]{1,0:T(8,128)(2,1)}), bf16[96,3072]{1,0:T(8,128)(2,1)}) %all-reduce.2.cloned.1.call-update) | async-done | bytes 589840 | tf_op jit(solution)/shard_map/psum | solution.py:131
  584.5 2.2 convert_element_type.81
  586.7 59.4 %all-to-all-done = bf16[8,2,256,1536]{2,3,1,0:T(8,128)(2,1)} async-done(((bf16[8,2,256,1536]{2,3,1,0:T(8,128)(2,1)}), bf16[8,2,256,1536]{2,3,1,0:T(8,128)(2,1)}, u32[]{:S(2)}, u32[]{:S(2)}) %all-to-all-start) | async-done | bytes 12582944 | tf_op jit(solution)/shard_map/all_to_all | solution.py:29
  646.1 6.8 %reduce.1 = bf16[2,256,1536]{1,2,0:T(8,128)(2,1)S(1)} reduce(bf16[8,2,256,1536]{2,3,1,0:T(8,128)(2,1)} %all-to-all-done, bf16[]{:T(256)} %constant.32.clone.1), dimensions={0}, to_apply=%region_5.6.clone | reduce | flops 5505024 | bytes 14155778 | tf_op jit(solution)/shard_map/reduce_sum | solution.py:30
  654.2 2.3 copy.55
  656.5 2.3 copy.54
  (32 shorter events, 11.9 us)
Async XLA Ops:
  7.2 62.2 %copy-start = (bf16[1,256,3072]{2,1,0:T(8,128)(2,1)S(1)}, bf16[1,256,3072]{2,1,0:T(8,128)(2,1)}, u32[]{:S(2)}) copy-start(bf16[1,256,3072]{2,1,0:T(8,128)(2,1)} %param.10) | copy-start | bytes 4718596
  7.2 62.1 %all-gather.5.cloned.1.call-start = ((), (), s32[]{:S(2)}) async-start(), calls=%async_computation.3 | async-start | bytes 10027008 | tf_op jit(solution)/shard_map/all_gather | solution.py:58
  7.9 217.7 %all-gather.3.cloned.1.call-start = ((), (), s32[]{:S(2)}) async-start(), calls=%async_computation.2 | async-start | bytes 14155776 | tf_op jit(solution)/shard_map/all_gather | solution.py:14
  79.3 157.0 %copy-start.3 = (bf16[3,256,4,128]{1,3,2,0:T(8,128)(2,1)S(1)}, bf16[3,256,4,128]{1,3,2,0:T(8,128)(2,1)}, u32[]{:S(2)}) copy-start(bf16[3,256,4,128]{1,3,2,0:T(8,128)(2,1)} %custom-call) | copy-start | bytes 2359300
  239.1 5.8 copy-start.1
  264.1 6.5 copy-start.2
  280.8 5.8 copy-start.1
  305.8 6.5 copy-start.2
  322.5 5.8 copy-start.1
  347.4 6.5 copy-start.2
  366.3 111.4 %all-to-all-start.1 = ((bf16[16,96,3072]{2,1,0:T(8,128)(2,1)}), bf16[16,96,3072]{2,1,0:T(8,128)(2,1)}, u32[]{:S(2)}, u32[]{:S(2)}) async-start(bf16[16,96,3072]{2,1,0:T(8,128)(2,1)} %bitcast.137), calls=%async_computation.1 | async-start | bytes 18874368 | tf_op jit(solution)/shard_map/all_to_all | solution.py:29
  477.7 168.4 %all-to-all-start = ((bf16[8,2,256,1536]{2,3,1,0:T(8,128)(2,1)}), bf16[8,2,256,1536]{2,3,1,0:T(8,128)(2,1)}, u32[]{:S(2)}, u32[]{:S(2)}) async-start(bf16[8,2,256,1536]{2,3,1,0:T(8,128)(2,1)} %copy.52), calls=%async_computation | async-start | bytes 25165824 | tf_op jit(solution)/shard_map/all_to_all | solution.py:29
  483.1 6.9 %copy-start.4 = (bf16[3,256,4,128]{1,3,2,0:T(8,128)(2,1)S(1)}, bf16[3,256,4,128]{1,3,2,0:T(8,128)(2,1)}, u32[]{:S(2)}) copy-start(bf16[3,256,4,128]{1,3,2,0:T(8,128)(2,1)} %get-tuple-element.54) | copy-start | bytes 2359300
  483.1 101.4 %all-reduce.2.cloned.1.call-start = ((), (), s32[]{:S(2)}) async-start(), calls=%async_computation.4 | async-start | bytes 1179648 | tf_op jit(solution)/shard_map/psum | solution.py:131
Sparse Core Ops, SparseCore 0:
  9.7 59.5 all-gather.4
  71.5 154.0 all-gather.2
  490.1 94.3 all-reduce.1
where the time goes:
time: 666 us; the launch traced here: 665 us
  waiting for transfers between devices  442 us (66%)
  matrix products  113 us (17%)
  local copies, waits for them, and re-layouts  49.6 us (7%)
  other arithmetic  36.1 us (5%)
  between operations  13.9 us (2%)
  starting transfers between devices  10.6 us (2%)
    all_gather x1, waiting for transfers between devices, in_one_piece(): result, at, outs = (lax.all_gather(both, axis, axis=dim, tiled=True), 0, [])  146 us
    all_to_all x2, waiting for transfers between devices, sent_and_summed(): lax.all_to_all(cut_along(array, dim, devices), axis, 0, 0, tiled=True)  146 us
    psum x1, waiting for transfers between devices, local(): lax.psum(partial_grad.astype(jnp.bfloat16), 'rows').astype(jnp.float32)  93.4 us
    all_gather x1, waiting for transfers between devices, local(): lax.all_gather(w_out, 'fsdp', axis=0, tiled=True)  55.7 us
    dot_general x3, matrix products, attend(): jnp.einsum('hqk,qhd->khd', probs_low, grad_heads, preferred_element_type=...  30.1 us
    dot_general x3, matrix products, attend(): jnp.einsum('hqk,khd->qhd', probs_low, value_heads, preferred_element_type...  27.3 us
    unnamed x13, local copies, waits for them, and re-layouts  19.9 us
    dot_general x3, matrix products, attend(): jnp.einsum('qhd,khd->hqk', grad_heads, value_heads, preferred_element_typ...  16.8 us
  transfers between devices with their start and end apart: 5, of which 5 were waited for; matrix products, arithmetic and copies ran while one was open for 7% of the time, Pallas kernels for 0%

commit v1 on v0

--- a/solution.py
+++ b/solution.py
@@ -55,7 +55,9 @@
     groups = HEADS // 4
     grad_attn = lax.dot_general(
         grad_flat,
-        lax.all_gather(w_out, "fsdp", axis=0, tiled=True),
+        jnp.concatenate(
+            lax.all_to_all(jnp.stack([w_out] * lax.axis_size("fsdp")), "fsdp", 0, 0), axis=0
+        ),
         (((1,), (1,)), ((), ())),
         preferred_element_type=jnp.float32,
     ).astype(jnp.bfloat16)

time: 666 us -> 677 us (1.017)
    all_to_all x0 -> x1, waiting for transfers between devices: none -> 174 us  [local(): lax.all_to_all(jnp.stack([w_out] * lax.axis_size('fsdp')), 'fsdp', 0, 0)]
    all_gather x1, waiting for transfers between devices: 146 us -> 27.6 us  [in_one_piece(): result, at, outs = (lax.all_gather(both, axis, axis=dim, tiled=True), 0, [])]
    all_gather x1 -> x0, waiting for transfers between devices: 55.7 us -> none  [local(): lax.all_gather(w_out, 'fsdp', axis=0, tiled=True)]
    unnamed x13 -> x15, local copies, waits for them, and re-layouts: 19.9 us -> 18.8 us
where the time goes in v1:
time: 677 us; the launch traced here: 676 us
  waiting for transfers between devices  441 us (65%)
  matrix products  113 us (17%)
  local copies, waits for them, and re-layouts  54.2 us (8%)
  other arithmetic  36.1 us (5%)
  starting transfers between devices  17.2 us (3%)
  between operations  14.2 us (2%)
    all_to_all x1, waiting for transfers between devices, local(): lax.all_to_all(jnp.stack([w_out] * lax.axis_size('fsdp')), 'fsdp', 0, 0)  174 us
    all_to_all x2, waiting for transfers between devices, sent_and_summed(): lax.all_to_all(cut_along(array, dim, devices), axis, 0, 0, tiled=True)  146 us
    psum x1, waiting for transfers between devices, local(): lax.psum(partial_grad.astype(jnp.bfloat16), 'rows').astype(jnp.float32)  93.4 us
    dot_general x3, matrix products, attend(): jnp.einsum('hqk,qhd->khd', probs_low, grad_heads, preferred_element_type=...  30.1 us
    all_gather x1, waiting for transfers between devices, in_one_piece(): result, at, outs = (lax.all_gather(both, axis, axis=dim, tiled=True), 0, [])  27.6 us
    dot_general x3, matrix products, attend(): jnp.einsum('hqk,khd->qhd', probs_low, value_heads, preferred_element_type...  27.3 us
    unnamed x15, local copies, waits for them, and re-layouts  18.8 us
    dot_general x3, matrix products, attend(): jnp.einsum('qhd,khd->hqk', grad_heads, value_heads, preferred_element_typ...  16.8 us
  transfers between devices with their start and end apart: 5, of which 5 were waited for; matrix products, arithmetic and copies ran while one was open for 7% of the time, Pallas kernels for 0%

profile of v1, /device:TPU:0, one launch (start us, length us, event | category | flops | bytes accessed | tf_op | source)
XLA Modules:
  0.0 676.0 jit_solution(1857903228667347604)
XLA Ops:
  7.2 1.5 copy.45
  8.7 1.4 copy.46
  11.5 5.9 stack.2
  17.4 6.6 all-to-all-start
  24.3 174.3 %all-to-all-done = bf16[16,96,3072]{2,1,0:T(8,128)(2,1)} async-done(((bf16[16,96,3072]{2,1,0:T(8,128)(2,1)}), bf16[16,96,3072]{2,1,0:T(8,128)(2,1)}, u32[]{:S(2)}, u32[]{:S(2)}) %all-to-all-start) | async-done | bytes 9437216 | tf_op jit(solution)/shard_map/all_to_all | solution.py:59
  198.6 7.2 %convolution_convert_fusion.1 = bf16[256,1536]{1,0:T(8,128)(2,1)} fusion(bf16[1536,3072]{1,0:T(8,128)(2,1)} %bitcast.19, bf16[1,256,3072]{2,1,0:T(8,128)(2,1)S(1)} %copy-done), kind=kOutput, calls=%fused_computation.48 | convolution fusion | flops 2416312320 | bytes 11796480 | tf_op jit(solution)/shard_map/dot_general | solution.py:56
  205.8 1.7 reshape.57
  208.6 27.6 %all-gather.2.cloned.1.call-done = bf16[2,2048,1536]{1,2,0:T(8,128)(2,1)} async-done(((bf16[2,256,1536]{1,2,0:T(8,128)(2,1)}), bf16[2,2048,1536]{1,2,0:T(8,128)(2,1)}) %all-gather.2.cloned.1.call-update) | async-done | bytes 12582928 | tf_op jit(solution)/shard_map/all_gather | solution.py:14
  236.2 10.6 %fusion.72 = (bf16[1,2048,1536]{1,2,0:T(8,128)(2,1)}, bf16[1,2048,1536]{1,2,0:T(8,128)(2,1)}) fusion(bf16[2,2048,1536]{1,2,0:T(8,128)(2,1)} %all-gather.2.cloned.1.call-done), kind=kLoop, calls=%fused_computation.54 | loop fusion | bytes 25165824 | tf_op jit(solution)/shard_map/slice | solution.py:16
  246.8 124.8 %while.16 = (s32[]{:T(128)}, bf16[3,256,4,128]{1,3,2,0:T(8,128)(2,1)S(1)}, bf16[3,256,4,128]{1,3,2,0:T(8,128)(2,1)}, bf16[3,2048,4,128]{1,3,2,0:T(8,128)(2,1)}, ...) while((s32[]{:T(128)}, ...), condition=%wide.region_4.5_spmd, body=%wide.region_0.4_spmd.sunk | while | flops 3266714624 | bytes 190351520 | solution.py:101
  246.8 2.9 fusion.106
  249.7 4.6 fusion.107
  255.4 9.1 %fusion.108 = bf16[3,256,4,128]{1,3,2,0:T(8,128)(2,1)S(1)} fusion(bf16[3,256,4,128]{1,3,2,0:T(8,128)(2,1)S(1)} %get-tuple-element.193, s32[]{:T(128)S(6)} %copy.79, bf16[3,2048,4,128]{1,3,2,0:T(8,128)(2,1)} %get-tuple-element.207, f32[4,256]{1,0:T(4,128)S(1)} %get-tuple-element.178, f32[4,256,2048]{2,1,0:T(8,128)} %copy-done.1), kind=kOutput, calls=%fused_computation.30.clone.1 | convolution fusion | flops 547490816 | bytes 19141632 | tf_op jit(solution)/shard_map/while/body/eval_jaxpr/hqk,khd->qhd/dot_general | solution.py:75
  264.5 10.0 %bitcast_dynamic-update-slice_fusion.5 = bf16[3,2048,4,128]{1,3,2,0:T(8,128)(2,1)} fusion(bf16[3,2048,4,128]{1,3,2,0:T(8,128)(2,1)} %get-tuple-element.196, s32[]{:T(128)S(6)} %copy.79, bf16[3,256,4,128]{3,1,2,0:T(8,128)(2,1)} %get-tuple-element.210, f32[4,256]{1,0:T(4,128)S(1)} %get-tuple-element.178, f32[4,256,2048]{2,1,0:T(8,128)} %copy-done.1), kind=kOutput, calls=%fused_computation.6.clone.1 | convolution fusion | flops 547359744 | bytes 21238784 | tf_op jit(solution)/shard_map/while/body/eval_jaxpr/hqk,qhd->khd/dot_general | solution.py:78
  274.6 5.6 multiply_reduce_fusion.3
  281.0 1.4 multiply_convert_fusion.2
  282.4 3.8 fusion.109
  286.2 2.2 bitcast_dynamic-update-slice_fusion.4
  288.4 2.9 fusion.106
  291.3 4.6 fusion.107
  297.0 9.1 %fusion.108 = bf16[3,256,4,128]{1,3,2,0:T(8,128)(2,1)S(1)} fusion(bf16[3,256,4,128]{1,3,2,0:T(8,128)(2,1)S(1)} %get-tuple-element.193, s32[]{:T(128)S(6)} %copy.79, bf16[3,2048,4,128]{1,3,2,0:T(8,128)(2,1)} %get-tuple-element.207, f32[4,256]{1,0:T(4,128)S(1)} %get-tuple-element.178, f32[4,256,2048]{2,1,0:T(8,128)} %copy-done.1), kind=kOutput, calls=%fused_computation.30.clone.1 | convolution fusion | flops 547490816 | bytes 19141632 | tf_op jit(solution)/shard_map/while/body/eval_jaxpr/hqk,khd->qhd/dot_general | solution.py:75
  306.1 10.0 %bitcast_dynamic-update-slice_fusion.5 = bf16[3,2048,4,128]{1,3,2,0:T(8,128)(2,1)} fusion(bf16[3,2048,4,128]{1,3,2,0:T(8,128)(2,1)} %get-tuple-element.196, s32[]{:T(128)S(6)} %copy.79, bf16[3,256,4,128]{3,1,2,0:T(8,128)(2,1)} %get-tuple-element.210, f32[4,256]{1,0:T(4,128)S(1)} %get-tuple-element.178, f32[4,256,2048]{2,1,0:T(8,128)} %copy-done.1), kind=kOutput, calls=%fused_computation.6.clone.1 | convolution fusion | flops 547359744 | bytes 21238784 | tf_op jit(solution)/shard_map/while/body/eval_jaxpr/hqk,qhd->khd/dot_general | solution.py:78
  316.1 5.6 multiply_reduce_fusion.3
  322.6 1.4 multiply_convert_fusion.2
  324.0 3.8 fusion.109
  327.8 2.2 bitcast_dynamic-update-slice_fusion.4
  330.0 2.9 fusion.106
  332.9 4.6 fusion.107
  338.6 9.1 %fusion.108 = bf16[3,256,4,128]{1,3,2,0:T(8,128)(2,1)S(1)} fusion(bf16[3,256,4,128]{1,3,2,0:T(8,128)(2,1)S(1)} %get-tuple-element.193, s32[]{:T(128)S(6)} %copy.79, bf16[3,2048,4,128]{1,3,2,0:T(8,128)(2,1)} %get-tuple-element.207, f32[4,256]{1,0:T(4,128)S(1)} %get-tuple-element.178, f32[4,256,2048]{2,1,0:T(8,128)} %copy-done.1), kind=kOutput, calls=%fused_computation.30.clone.1 | convolution fusion | flops 547490816 | bytes 19141632 | tf_op jit(solution)/shard_map/while/body/eval_jaxpr/hqk,khd->qhd/dot_general | solution.py:75
  347.7 10.1 %bitcast_dynamic-update-slice_fusion.5 = bf16[3,2048,4,128]{1,3,2,0:T(8,128)(2,1)} fusion(bf16[3,2048,4,128]{1,3,2,0:T(8,128)(2,1)} %get-tuple-element.196, s32[]{:T(128)S(6)} %copy.79, bf16[3,256,4,128]{3,1,2,0:T(8,128)(2,1)} %get-tuple-element.210, f32[4,256]{1,0:T(4,128)S(1)} %get-tuple-element.178, f32[4,256,2048]{2,1,0:T(8,128)} %copy-done.1), kind=kOutput, calls=%fused_computation.6.clone.1 | convolution fusion | flops 547359744 | bytes 21238784 | tf_op jit(solution)/shard_map/while/body/eval_jaxpr/hqk,qhd->khd/dot_general | solution.py:78
  357.8 5.6 multiply_reduce_fusion.3
  364.3 1.4 multiply_convert_fusion.2
  365.6 3.8 fusion.109
  369.5 2.1 bitcast_dynamic-update-slice_fusion.4
  371.6 5.1 convolution_convert_fusion
  376.7 4.8 all-to-all-start.2
  381.6 5.5 copy.67
  387.1 5.5 copy.66
  393.9 7.8 %copy.52 = bf16[8,2,256,1536]{2,3,1,0:T(8,128)(2,1)} copy(bf16[8,2,256,1536]{2,0,3,1:T(8,128)(2,1)S(1)} %maximum_bitcast_fusion) | data formatting | bytes 25165824 | tf_op jit(solution)/shard_map/transpose | solution.py:24
  401.7 86.4 %all-to-all-done.2 = bf16[16,96,3072]{2,1,0:T(8,128)(2,1)} async-done(((bf16[16,96,3072]{2,1,0:T(8,128)(2,1)}), bf16[16,96,3072]{2,1,0:T(8,128)(2,1)}, u32[]{:S(2)}, u32[]{:S(2)}) %all-to-all-start.2) | async-done | bytes 9437216 | tf_op jit(solution)/shard_map/all_to_all | solution.py:29
  488.1 5.4 all-to-all-start.1
  493.8 6.5 reduce_sum.40
  501.6 93.4 %all-reduce.2.cloned.1.call-done = bf16[96,3072]{1,0:T(8,128)(2,1)} async-done(((bf16[96,3072]{1,0:T(8,128)(2,1)}), bf16[96,3072]{1,0:T(8,128)(2,1)}) %all-reduce.2.cloned.1.call-update) | async-done | bytes 589840 | tf_op jit(solution)/shard_map/psum | solution.py:133
  594.9 2.2 convert_element_type.81
  597.1 59.4 %all-to-all-done.1 = bf16[8,2,256,1536]{2,3,1,0:T(8,128)(2,1)} async-done(((bf16[8,2,256,1536]{2,3,1,0:T(8,128)(2,1)}), bf16[8,2,256,1536]{2,3,1,0:T(8,128)(2,1)}, u32[]{:S(2)}, u32[]{:S(2)}) %all-to-all-start.1) | async-done | bytes 12582944 | tf_op jit(solution)/shard_map/all_to_all | solution.py:29
  656.5 6.8 %reduce.1 = bf16[2,256,1536]{1,2,0:T(8,128)(2,1)S(1)} reduce(bf16[8,2,256,1536]{2,3,1,0:T(8,128)(2,1)} %all-to-all-done.1, bf16[]{:T(256)} %constant.32.clone.1), dimensions={0}, to_apply=%region_5.6.clone | reduce | flops 5505024 | bytes 14155778 | tf_op jit(solution)/shard_map/reduce_sum | solution.py:30
  664.6 2.3 copy.55
  666.9 2.3 copy.54
  (34 shorter events, 12.5 us)
Async XLA Ops:
  7.2 191.5 %copy-start = (bf16[1,256,3072]{2,1,0:T(8,128)(2,1)S(1)}, bf16[1,256,3072]{2,1,0:T(8,128)(2,1)}, u32[]{:S(2)}) copy-start(bf16[1,256,3072]{2,1,0:T(8,128)(2,1)} %param.10) | copy-start | bytes 4718596
  7.2 229.0 %all-gather.2.cloned.1.call-start = ((), (), s32[]{:S(2)}) async-start(), calls=%async_computation.3 | async-start | bytes 14155776 | tf_op jit(solution)/shard_map/all_gather | solution.py:14
  17.4 6.7 copy-start.4
  17.4 181.2 %all-to-all-start = ((bf16[16,96,3072]{2,1,0:T(8,128)(2,1)}), bf16[16,96,3072]{2,1,0:T(8,128)(2,1)}, u32[]{:S(2)}, u32[]{:S(2)}) async-start(bf16[16,96,3072]{2,1,0:T(8,128)(2,1)} %stack.2), calls=%async_computation | async-start | bytes 18874368 | tf_op jit(solution)/shard_map/all_to_all | solution.py:59
  208.6 38.2 %copy-start.3 = (bf16[3,256,4,128]{1,3,2,0:T(8,128)(2,1)S(1)}, bf16[3,256,4,128]{1,3,2,0:T(8,128)(2,1)}, u32[]{:S(2)}) copy-start(bf16[3,256,4,128]{1,3,2,0:T(8,128)(2,1)} %custom-call) | copy-start | bytes 2359300
  249.7 5.7 copy-start.1
  274.6 6.5 copy-start.2
  291.3 5.7 copy-start.1
  316.1 6.5 copy-start.2
  332.9 5.7 copy-start.1
  357.8 6.5 copy-start.2
  376.7 111.4 %all-to-all-start.2 = ((bf16[16,96,3072]{2,1,0:T(8,128)(2,1)}), bf16[16,96,3072]{2,1,0:T(8,128)(2,1)}, u32[]{:S(2)}, u32[]{:S(2)}) async-start(bf16[16,96,3072]{2,1,0:T(8,128)(2,1)} %bitcast.138), calls=%async_computation.2 | async-start | bytes 18874368 | tf_op jit(solution)/shard_map/all_to_all | solution.py:29
  488.1 168.4 %all-to-all-start.1 = ((bf16[8,2,256,1536]{2,3,1,0:T(8,128)(2,1)}), bf16[8,2,256,1536]{2,3,1,0:T(8,128)(2,1)}, u32[]{:S(2)}, u32[]{:S(2)}) async-start(bf16[8,2,256,1536]{2,3,1,0:T(8,128)(2,1)} %copy.52), calls=%async_computation.1 | async-start | bytes 25165824 | tf_op jit(solution)/shard_map/all_to_all | solution.py:29
  493.5 6.9 %copy-start.5 = (bf16[3,256,4,128]{1,3,2,0:T(8,128)(2,1)S(1)}, bf16[3,256,4,128]{1,3,2,0:T(8,128)(2,1)}, u32[]{:S(2)}) copy-start(bf16[3,256,4,128]{1,3,2,0:T(8,128)(2,1)} %get-tuple-element.54) | copy-start | bytes 2359300
  493.5 101.4 %all-reduce.2.cloned.1.call-start = ((), (), s32[]{:S(2)}) async-start(), calls=%async_computation.4 | async-start | bytes 1179648 | tf_op jit(solution)/shard_map/psum | solution.py:133
Sparse Core Ops, SparseCore 0:
  11.6 224.5 all-gather.1
  500.5 94.3 all-reduce.1
